TPU v7x, 128 devices: a whole 4x4x4 slice. The times are simulated.
128 devices in a mesh: chan: 2 (over x_hi), blk: 64 (over y, z, x_lo, core).
Axes of the slice: x: 4 (x_hi: 2, x_lo: 2; x = x_hi * 2 + x_lo), y: 4, z: 4, core: 2. Of those that a mesh axis runs over, the one named last changes fastest.
Arguments:
- features: bfloat16 [64, 2, 256, 128], P('blk', 'chan'), may hold values from -6 to 6
- transforms: bfloat16 [8, 128, 128], replicated, may hold values from -0.5 to 0.5
- self_weight: bfloat16 [128, 128], replicated, may hold values from -0.5 to 0.5
- tile_rows: int32 [8, 64, 64, 8], P('chan', 'blk'), may hold values from 0 to 3
- tile_cols: int32 [8, 64, 64, 8], P('chan', 'blk'), may hold values from 0 to 3
- tile_ids: int32 [8, 64, 64, 8], P('chan', 'blk'), may hold values from 0 to 31
- tile_count: int32 [8, 64, 64], P('chan', 'blk'), may hold values from 0 to 8
- tile_pool: bfloat16 [8, 64, 32, 128, 128], P('chan', 'blk'), may hold values from -0.0234375 to 0.0234375
Outputs:
- updated: bfloat16 [64, 2, 256, 128], P('blk', 'chan')
All inputs are finite; a program needn't handle non-finite values.
Results may differ from a plain program's by a relative error of at most 0.0041.
Values may be sent and summed in bfloat16 or wider, within the bound.
No kernel may reach another device: no remote copies, remote signals or barrier semaphores. Data moves between devices by JAX's collectives and lax.ppermute only.
A program may use at most 128 MiB of HBM per device.

v0:
```python
import math
import jax
import jax.numpy as jnp
from jax import lax
from jax.sharding import PartitionSpec as P


def shards(
    features, transforms, self_weight, tile_rows, tile_cols, tile_ids, tile_count, tile_pool
):
    chan_count = lax.axis_size("chan")
    chan_index = lax.axis_index("chan")
    own_rows = features[0, 0]
    half_rows = own_rows.shape[0]
    width = own_rows.shape[1]
    tile_size = tile_pool.shape[-1]
    pool_size = tile_pool.shape[2]
    block_rows = half_rows * chan_count
    tiles_block = block_rows // tile_size
    rel_dev = transforms.shape[0] // chan_count
    slot_count = tile_rows.shape[-1]
    rows_list = tile_rows[:, 0]
    cols_list = tile_cols[:, 0]
    ids_list = tile_ids[:, 0]
    count_list = tile_count[:, 0]
    pool_flat = tile_pool[:, 0].reshape(rel_dev, pool_size, tile_size * tile_size)
    slot_range = jnp.arange(slot_count)
    tile_range = jnp.arange(tiles_block)
    pool_range = jnp.arange(pool_size)

    def apply_group(total, hidden_group, first):
        group = hidden_group.shape[1]
        cols_now = lax.dynamic_slice_in_dim(cols_list, first, group, 1)
        rows_now = lax.dynamic_slice_in_dim(rows_list, first, group, 1)
        ids_now = lax.dynamic_slice_in_dim(ids_list, first, group, 1)
        count_now = lax.dynamic_slice_in_dim(count_list, first, group, 1)
        pick_cols = (cols_now[..., None] == tile_range).astype(jnp.bfloat16)
        flat_hidden = hidden_group.reshape(rel_dev, group, tiles_block, tile_size * width)
        picked = jnp.einsum(
            "rgks,rgsx->rgkx", pick_cols, flat_hidden, preferred_element_type=jnp.float32
        ).astype(jnp.bfloat16)
        picked = picked.reshape(rel_dev, group, slot_count, tile_size, width)
        pick_ids = (ids_now[..., None] == pool_range).astype(jnp.bfloat16)
        weights = jnp.einsum(
            "rgkp,rpx->rgkx", pick_ids, pool_flat, preferred_element_type=jnp.float32
        ).astype(jnp.bfloat16)
        weights = weights.reshape(rel_dev, group, slot_count, tile_size, tile_size)
        product = jnp.einsum(
            "rgkab,rgkbd->rgkad", weights, picked, preferred_element_type=jnp.float32
        )
        live = (slot_range < count_now[..., None]).astype(jnp.float32)
        onehot = (rows_now[..., None] == tile_range).astype(jnp.float32) * live[..., None]
        return total + jnp.einsum(
            "rgkt,rgkad->tad", onehot, product, precision=lax.Precision.HIGHEST
        )

    empty = jnp.zeros((tiles_block, tile_size, width), jnp.float32)
    all_hidden = jnp.einsum(
        "nd,rde->rne", own_rows, transforms, preferred_element_type=jnp.float32
    ).astype(jnp.bfloat16)
    mine = lax.all_to_all(all_hidden, "chan", split_axis=0, concat_axis=1, tiled=True)
    piece = lax.all_gather(mine, "blk", axis=1, tiled=True)
    blocks_here = piece.shape[1] // block_rows

    def fetch(offset, group):
        part_rows = lax.dynamic_slice_in_dim(piece, offset * block_rows, group * block_rows, 1)
        return part_rows.reshape(rel_dev, group, tiles_block, tile_size, width)

    group = math.gcd(blocks_here, 4)
    turns = blocks_here // group

    def step_once(turn, carry):
        return apply_group(carry, fetch(turn * group, group), turn * group)

    agg = lax.fori_loop(0, turns, step_once, empty)
    partial_rows = agg.reshape(block_rows, width)
    summed = lax.psum(partial_rows, "chan")
    share = lax.dynamic_slice_in_dim(summed, chan_index * half_rows, half_rows, 0)
    selfterm = jnp.dot(own_rows, self_weight, preferred_element_type=jnp.float32)
    updated = jax.nn.relu(selfterm + share).astype(jnp.bfloat16)
    return updated.reshape(1, 1, half_rows, width)


def solution(mesh):
    placed = (
        P("blk", "chan", None, None),
        P(),
        P(),
        P("chan", "blk", None, None),
        P("chan", "blk", None, None),
        P("chan", "blk", None, None),
        P("chan", "blk", None),
        P("chan", "blk", None, None, None),
    )
    return jax.shard_map(
        shards, mesh=mesh, in_specs=placed, out_specs=P("blk", "chan", None, None), check_vma=False
    )
```

profile of v0, /device:TPU:1, one launch (start us, length us, event | category | flops | bytes accessed | tf_op | source)
XLA Modules:
  0.0 706.5 jit_solution(2026471395278241592)
XLA Ops:
  8.7 13.2 %all_to_all.18 = bf16[8,256,128]{1,2,0:T(8,128)(2,1)S(1)} all-to-all(bf16[8,256,128]{1,2,0:T(8,128)(2,1)S(1)} %fusion.31), channel_id=1, replica_groups=mesh['chan'=2,'blk'=64] {'chan'}, dimensions={0} | all-to-all | bytes 1048576 | tf_op jit(solution)/shard_map/all_to_all | solution.py:61
  23.0 7.3 %reshape_squeeze.3 = bf16[4,32,16384]{2,1,0:T(8,128)(2,1)} reshape(bf16[4,1,32,128,128]{4,3,2,1,0:T(8,128)(2,1)} %param.17) | data formatting | bytes 8388608 | tf_op jit(solution)/shard_map/reshape;squeeze | solution.py:26
  30.8 181.1 %all-gather.2.cloned.1.call-done = bf16[4,32768,128]{2,1,0:T(8,128)(2,1)} async-done(((bf16[4,512,128]{2,1,0:T(8,128)(2,1)}), bf16[4,32768,128]{2,1,0:T(8,128)(2,1)}) %all-gather.2.cloned.1.call-update) | async-done | bytes 33554448 | tf_op jit(solution)/shard_map/all_gather | solution.py:62
  211.9 453.9 %while.17 = (s32[]{:T(128)}, f32[4,128,128]{2,0,1:T(4,128)S(1)}, s32[4,64,8]{2,0,1:T(4,128)S(1)}, s32[4,64]{0,1:T(8,128)S(1)}, s32[4,64,8]{2,1,0:T(8,128)S(1)}, ...) while((s32[]{:T(128)}, f32[4,128,128]{2,0,1:T(4,128)S(1)}, ...), condition=%wide.region_1.0_spmd.clone.clone, body=%wide.region_0.0_spmd.clone.clone.sunk | while | flops 792860416 | bytes 65542100 | solution.py:75
  221.1 4.5 fusion.61
  225.6 14.6 %fusion.63 = f32[4,128,128]{2,0,1:T(4,128)S(1)} fusion(f32[4,4,8,128,128]{4,3,2,1,0:T(8,128)} %fusion.61, f32[4,128,128]{2,0,1:T(4,128)S(1)} %get-tuple-element.418, pred[]{:T(512)S(6)} %compare.3, f32[4,4,8]{2,0,1:T(4,128)S(1)} %fusion.62, s32[4,4,8]{2,0,1:T(4,128)S(1)} %get-tuple-element.402), kind=kOutput, calls=%fused_computation.14.clone.1 | convolution fusion | flops 100795392 | bytes 8913921 | tf_op jit(solution)/shard_map/while/body/eval_jaxpr/rgkt,rgkad->tad/dot_general | solution.py:53
  249.4 4.5 fusion.61
  254.0 14.6 %fusion.63 = f32[4,128,128]{2,0,1:T(4,128)S(1)} fusion(f32[4,4,8,128,128]{4,3,2,1,0:T(8,128)} %fusion.61, f32[4,128,128]{2,0,1:T(4,128)S(1)} %get-tuple-element.418, pred[]{:T(512)S(6)} %compare.3, f32[4,4,8]{2,0,1:T(4,128)S(1)} %fusion.62, s32[4,4,8]{2,0,1:T(4,128)S(1)} %get-tuple-element.402), kind=kOutput, calls=%fused_computation.14.clone.1 | convolution fusion | flops 100795392 | bytes 8913921 | tf_op jit(solution)/shard_map/while/body/eval_jaxpr/rgkt,rgkad->tad/dot_general | solution.py:53
  282.3 14.6 %fusion.63 = f32[4,128,128]{2,0,1:T(4,128)S(1)} fusion(f32[4,4,8,128,128]{4,3,2,1,0:T(8,128)} %fusion.61, f32[4,128,128]{2,0,1:T(4,128)S(1)} %get-tuple-element.418, pred[]{:T(512)S(6)} %compare.3, f32[4,4,8]{2,0,1:T(4,128)S(1)} %fusion.62, s32[4,4,8]{2,0,1:T(4,128)S(1)} %get-tuple-element.402), kind=kOutput, calls=%fused_computation.14.clone.1 | convolution fusion | flops 100795392 | bytes 8913921 | tf_op jit(solution)/shard_map/while/body/eval_jaxpr/rgkt,rgkad->tad/dot_general | solution.py:53
  306.2 4.5 fusion.61
  310.7 14.6 %fusion.63 = f32[4,128,128]{2,0,1:T(4,128)S(1)} fusion(f32[4,4,8,128,128]{4,3,2,1,0:T(8,128)} %fusion.61, f32[4,128,128]{2,0,1:T(4,128)S(1)} %get-tuple-element.418, pred[]{:T(512)S(6)} %compare.3, f32[4,4,8]{2,0,1:T(4,128)S(1)} %fusion.62, s32[4,4,8]{2,0,1:T(4,128)S(1)} %get-tuple-element.402), kind=kOutput, calls=%fused_computation.14.clone.1 | convolution fusion | flops 100795392 | bytes 8913921 | tf_op jit(solution)/shard_map/while/body/eval_jaxpr/rgkt,rgkad->tad/dot_general | solution.py:53
  334.5 4.5 fusion.61
  339.1 14.6 %fusion.63 = f32[4,128,128]{2,0,1:T(4,128)S(1)} fusion(f32[4,4,8,128,128]{4,3,2,1,0:T(8,128)} %fusion.61, f32[4,128,128]{2,0,1:T(4,128)S(1)} %get-tuple-element.418, pred[]{:T(512)S(6)} %compare.3, f32[4,4,8]{2,0,1:T(4,128)S(1)} %fusion.62, s32[4,4,8]{2,0,1:T(4,128)S(1)} %get-tuple-element.402), kind=kOutput, calls=%fused_computation.14.clone.1 | convolution fusion | flops 100795392 | bytes 8913921 | tf_op jit(solution)/shard_map/while/body/eval_jaxpr/rgkt,rgkad->tad/dot_general | solution.py:53
  367.5 14.6 %fusion.63 = f32[4,128,128]{2,0,1:T(4,128)S(1)} fusion(f32[4,4,8,128,128]{4,3,2,1,0:T(8,128)} %fusion.61, f32[4,128,128]{2,0,1:T(4,128)S(1)} %get-tuple-element.418, pred[]{:T(512)S(6)} %compare.3, f32[4,4,8]{2,0,1:T(4,128)S(1)} %fusion.62, s32[4,4,8]{2,0,1:T(4,128)S(1)} %get-tuple-element.402), kind=kOutput, calls=%fused_computation.14.clone.1 | convolution fusion | flops 100795392 | bytes 8913921 | tf_op jit(solution)/shard_map/while/body/eval_jaxpr/rgkt,rgkad->tad/dot_general | solution.py:53
  391.3 4.5 fusion.61
  395.8 14.6 %fusion.63 = f32[4,128,128]{2,0,1:T(4,128)S(1)} fusion(f32[4,4,8,128,128]{4,3,2,1,0:T(8,128)} %fusion.61, f32[4,128,128]{2,0,1:T(4,128)S(1)} %get-tuple-element.418, pred[]{:T(512)S(6)} %compare.3, f32[4,4,8]{2,0,1:T(4,128)S(1)} %fusion.62, s32[4,4,8]{2,0,1:T(4,128)S(1)} %get-tuple-element.402), kind=kOutput, calls=%fused_computation.14.clone.1 | convolution fusion | flops 100795392 | bytes 8913921 | tf_op jit(solution)/shard_map/while/body/eval_jaxpr/rgkt,rgkad->tad/dot_general | solution.py:53
  419.7 4.5 fusion.61
  424.2 14.6 %fusion.63 = f32[4,128,128]{2,0,1:T(4,128)S(1)} fusion(f32[4,4,8,128,128]{4,3,2,1,0:T(8,128)} %fusion.61, f32[4,128,128]{2,0,1:T(4,128)S(1)} %get-tuple-element.418, pred[]{:T(512)S(6)} %compare.3, f32[4,4,8]{2,0,1:T(4,128)S(1)} %fusion.62, s32[4,4,8]{2,0,1:T(4,128)S(1)} %get-tuple-element.402), kind=kOutput, calls=%fused_computation.14.clone.1 | convolution fusion | flops 100795392 | bytes 8913921 | tf_op jit(solution)/shard_map/while/body/eval_jaxpr/rgkt,rgkad->tad/dot_general | solution.py:53
  452.6 14.6 %fusion.63 = f32[4,128,128]{2,0,1:T(4,128)S(1)} fusion(f32[4,4,8,128,128]{4,3,2,1,0:T(8,128)} %fusion.61, f32[4,128,128]{2,0,1:T(4,128)S(1)} %get-tuple-element.418, pred[]{:T(512)S(6)} %compare.3, f32[4,4,8]{2,0,1:T(4,128)S(1)} %fusion.62, s32[4,4,8]{2,0,1:T(4,128)S(1)} %get-tuple-element.402), kind=kOutput, calls=%fused_computation.14.clone.1 | convolution fusion | flops 100795392 | bytes 8913921 | tf_op jit(solution)/shard_map/while/body/eval_jaxpr/rgkt,rgkad->tad/dot_general | solution.py:53
  476.4 4.5 fusion.61
  480.9 14.6 %fusion.63 = f32[4,128,128]{2,0,1:T(4,128)S(1)} fusion(f32[4,4,8,128,128]{4,3,2,1,0:T(8,128)} %fusion.61, f32[4,128,128]{2,0,1:T(4,128)S(1)} %get-tuple-element.418, pred[]{:T(512)S(6)} %compare.3, f32[4,4,8]{2,0,1:T(4,128)S(1)} %fusion.62, s32[4,4,8]{2,0,1:T(4,128)S(1)} %get-tuple-element.402), kind=kOutput, calls=%fused_computation.14.clone.1 | convolution fusion | flops 100795392 | bytes 8913921 | tf_op jit(solution)/shard_map/while/body/eval_jaxpr/rgkt,rgkad->tad/dot_general | solution.py:53
  504.8 4.5 fusion.61
  509.3 14.6 %fusion.63 = f32[4,128,128]{2,0,1:T(4,128)S(1)} fusion(f32[4,4,8,128,128]{4,3,2,1,0:T(8,128)} %fusion.61, f32[4,128,128]{2,0,1:T(4,128)S(1)} %get-tuple-element.418, pred[]{:T(512)S(6)} %compare.3, f32[4,4,8]{2,0,1:T(4,128)S(1)} %fusion.62, s32[4,4,8]{2,0,1:T(4,128)S(1)} %get-tuple-element.402), kind=kOutput, calls=%fused_computation.14.clone.1 | convolution fusion | flops 100795392 | bytes 8913921 | tf_op jit(solution)/shard_map/while/body/eval_jaxpr/rgkt,rgkad->tad/dot_general | solution.py:53
  537.7 14.6 %fusion.63 = f32[4,128,128]{2,0,1:T(4,128)S(1)} fusion(f32[4,4,8,128,128]{4,3,2,1,0:T(8,128)} %fusion.61, f32[4,128,128]{2,0,1:T(4,128)S(1)} %get-tuple-element.418, pred[]{:T(512)S(6)} %compare.3, f32[4,4,8]{2,0,1:T(4,128)S(1)} %fusion.62, s32[4,4,8]{2,0,1:T(4,128)S(1)} %get-tuple-element.402), kind=kOutput, calls=%fused_computation.14.clone.1 | convolution fusion | flops 100795392 | bytes 8913921 | tf_op jit(solution)/shard_map/while/body/eval_jaxpr/rgkt,rgkad->tad/dot_general | solution.py:53
  561.5 4.5 fusion.61
  566.0 14.6 %fusion.63 = f32[4,128,128]{2,0,1:T(4,128)S(1)} fusion(f32[4,4,8,128,128]{4,3,2,1,0:T(8,128)} %fusion.61, f32[4,128,128]{2,0,1:T(4,128)S(1)} %get-tuple-element.418, pred[]{:T(512)S(6)} %compare.3, f32[4,4,8]{2,0,1:T(4,128)S(1)} %fusion.62, s32[4,4,8]{2,0,1:T(4,128)S(1)} %get-tuple-element.402), kind=kOutput, calls=%fused_computation.14.clone.1 | convolution fusion | flops 100795392 | bytes 8913921 | tf_op jit(solution)/shard_map/while/body/eval_jaxpr/rgkt,rgkad->tad/dot_general | solution.py:53
  589.9 4.5 fusion.61
  594.4 14.6 %fusion.63 = f32[4,128,128]{2,0,1:T(4,128)S(1)} fusion(f32[4,4,8,128,128]{4,3,2,1,0:T(8,128)} %fusion.61, f32[4,128,128]{2,0,1:T(4,128)S(1)} %get-tuple-element.418, pred[]{:T(512)S(6)} %compare.3, f32[4,4,8]{2,0,1:T(4,128)S(1)} %fusion.62, s32[4,4,8]{2,0,1:T(4,128)S(1)} %get-tuple-element.402), kind=kOutput, calls=%fused_computation.14.clone.1 | convolution fusion | flops 100795392 | bytes 8913921 | tf_op jit(solution)/shard_map/while/body/eval_jaxpr/rgkt,rgkad->tad/dot_general | solution.py:53
  622.8 14.6 %fusion.63 = f32[4,128,128]{2,0,1:T(4,128)S(1)} fusion(f32[4,4,8,128,128]{4,3,2,1,0:T(8,128)} %fusion.61, f32[4,128,128]{2,0,1:T(4,128)S(1)} %get-tuple-element.418, pred[]{:T(512)S(6)} %compare.3, f32[4,4,8]{2,0,1:T(4,128)S(1)} %fusion.62, s32[4,4,8]{2,0,1:T(4,128)S(1)} %get-tuple-element.402), kind=kOutput, calls=%fused_computation.14.clone.1 | convolution fusion | flops 100795392 | bytes 8913921 | tf_op jit(solution)/shard_map/while/body/eval_jaxpr/rgkt,rgkad->tad/dot_general | solution.py:53
  646.6 4.5 fusion.61
  651.2 14.6 %fusion.63 = f32[4,128,128]{2,0,1:T(4,128)S(1)} fusion(f32[4,4,8,128,128]{4,3,2,1,0:T(8,128)} %fusion.61, f32[4,128,128]{2,0,1:T(4,128)S(1)} %get-tuple-element.418, pred[]{:T(512)S(6)} %compare.3, f32[4,4,8]{2,0,1:T(4,128)S(1)} %fusion.62, s32[4,4,8]{2,0,1:T(4,128)S(1)} %get-tuple-element.402), kind=kOutput, calls=%fused_computation.14.clone.1 | convolution fusion | flops 100795392 | bytes 8913921 | tf_op jit(solution)/shard_map/while/body/eval_jaxpr/rgkt,rgkad->tad/dot_general | solution.py:53
  666.5 31.5 %all-reduce.2.cloned.1.call-done = f32[512,128]{1,0:T(8,128)} async-done(((f32[512,128]{1,0:T(8,128)}), f32[512,128]{1,0:T(8,128)}) %all-reduce.2.cloned.1.call-update) | async-done | bytes 262160 | tf_op jit(solution)/shard_map/psum | solution.py:77
  (192 shorter events, 176.1 us)
Async XLA Ops:
  6.5 1.0 copy-start
  6.5 205.3 %all-gather.2.cloned.1.call-start = ((), (), s32[]{:S(2)}) async-start(), calls=%async_computation.1 | async-start | bytes 34078720 | tf_op jit(solution)/shard_map/all_gather | solution.py:62
  22.9 675.1 %all-reduce.2.cloned.1.call-start = ((), (), s32[]{:S(2)}) async-start(), calls=%async_computation.2 | async-start | bytes 524288 | tf_op jit(solution)/shard_map/psum | solution.py:77
  22.9 7.4 %copy-start.4 = (s32[4,1,64,8]{2,3,1,0:T(8,128)S(1)}, s32[4,1,64,8]{2,3,1,0:T(8,128)}, u32[]{:S(2)}) copy-start(s32[4,1,64,8]{2,3,1,0:T(8,128)} %param.13) | copy-start | bytes 24580
  23.0 7.5 %copy-start.5 = (s32[4,1,64,8]{2,3,1,0:T(8,128)S(1)}, s32[4,1,64,8]{2,3,1,0:T(8,128)}, u32[]{:S(2)}) copy-start(s32[4,1,64,8]{2,3,1,0:T(8,128)} %param.15) | copy-start | bytes 24580
  23.0 7.6 %copy-start.6 = (s32[4,1,64,8]{2,3,1,0:T(8,128)S(1)}, s32[4,1,64,8]{2,3,1,0:T(8,128)}, u32[]{:S(2)}) copy-start(s32[4,1,64,8]{2,3,1,0:T(8,128)} %param.14) | copy-start | bytes 24580
  23.0 7.7 %copy-start.7 = (s32[4,1,64]{2,1,0:T(1,128)S(1)}, s32[4,1,64]{2,1,0:T(1,128)}, u32[]{:S(2)}) copy-start(s32[4,1,64]{2,1,0:T(1,128)} %param.16) | copy-start | bytes 3076
  211.8 486.1 %copy-start.2 = (bf16[1,1,256,128]{3,2,1,0:T(8,128)(2,1)S(1)}, bf16[1,1,256,128]{3,2,1,0:T(8,128)(2,1)}, u32[]{:S(2)}) copy-start(bf16[1,1,256,128]{3,2,1,0:T(8,128)(2,1)} %param.10) | copy-start | bytes 196612
  211.9 486.1 %copy-start.3 = (bf16[128,128]{1,0:T(8,128)(2,1)S(1)}, bf16[128,128]{1,0:T(8,128)(2,1)}, u32[]{:S(2)}) copy-start(bf16[128,128]{1,0:T(8,128)(2,1)} %param.12) | copy-start | bytes 98308
  217.6 2.2 copy-start.1
  245.9 2.2 copy-start.1
  274.3 2.2 copy-start.1
  302.7 2.2 copy-start.1
  331.1 2.2 copy-start.1
  359.4 2.2 copy-start.1
  387.8 2.2 copy-start.1
  416.2 2.2 copy-start.1
  444.5 2.2 copy-start.1
  472.9 2.2 copy-start.1
  501.3 2.2 copy-start.1
  529.6 2.2 copy-start.1
  558.0 2.2 copy-start.1
  586.4 2.2 copy-start.1
  614.8 2.2 copy-start.1
  643.1 2.2 copy-start.1
Sparse Core Ops, SparseCore 0:
  23.0 188.7 all-gather.1
  666.6 31.2 all-reduce.1
where the time goes:
time: 709 us; the launch traced here: 706 us
  matrix products  357 us (50%)
  waiting for transfers between devices  213 us (30%)
  local copies, waits for them, and re-layouts  108 us (15%)
  between operations  13.5 us (2%)
  blocking collectives  13.2 us (2%)
    dot_general x16, matrix products, apply_group(): jnp.einsum('rgkt,rgkad->tad', onehot, product, precision=lax.Precision.HI...  233 us
    all_gather x1, waiting for transfers between devices, shards(): piece = lax.all_gather(mine, 'blk', axis=1, tiled=True)  181 us
    dot_general x16, matrix products, apply_group(): jnp.einsum('rgkab,rgkbd->rgkad', weights, picked, preferred_element_type=...  71.4 us
    dynamic_slice x16, local copies, waits for them, and re-layouts, fetch(): lax.dynamic_slice_in_dim(piece, offset * block_rows, group * block_rows, 1)  49 us
    reshape x16, local copies, waits for them, and re-layouts, apply_group(): hidden_group.reshape(rel_dev, group, tiles_block, tile_size * width)  42 us
    psum x1, waiting for transfers between devices, shards(): summed = lax.psum(partial_rows, 'chan')  31.5 us
    dot_general x16, matrix products, apply_group(): jnp.einsum('rgks,rgsx->rgkx', pick_cols, flat_hidden, preferred_element_t...  28.2 us
    dot_general x16, matrix products, apply_group(): jnp.einsum('rgkp,rpx->rgkx', pick_ids, pool_flat, preferred_element_type=...  20.7 us
  transfers between devices with their start and end apart: 2, of which 2 were waited for; matrix products, arithmetic and copies ran while one was open for 1% of the time, Pallas kernels for 0%

commit v1 on v0

--- a/solution.py
+++ b/solution.py
@@ -1,8 +1,16 @@
+import functools
 import math
 import jax
 import jax.numpy as jnp
 from jax import lax
 from jax.sharding import PartitionSpec as P
+
+
+def match_the_ends(inp, lane_axis):
+    return jnp.sum(lax.all_gather(inp, lane_axis), axis=0)
+
+
+balance_sample = functools.partial(match_the_ends, lane_axis="chan")
 
 
 def shards(
@@ -74,7 +82,7 @@
 
     agg = lax.fori_loop(0, turns, step_once, empty)
     partial_rows = agg.reshape(block_rows, width)
-    summed = lax.psum(partial_rows, "chan")
+    summed = balance_sample(partial_rows)
     share = lax.dynamic_slice_in_dim(summed, chan_index * half_rows, half_rows, 0)
     selfterm = jnp.dot(own_rows, self_weight, preferred_element_type=jnp.float32)
     updated = jax.nn.relu(selfterm + share).astype(jnp.bfloat16)

time: 709 us -> 686 us (0.968)
  waiting for transfers between devices: 213 us -> 181 us
  blocking collectives: 13.2 us -> 23 us
    psum x1 -> x0, waiting for transfers between devices: 31.5 us -> none  [shards(): summed = lax.psum(partial_rows, 'chan')]
    all_gather x0 -> x1, blocking collectives: none -> 9.81 us  [match_the_ends(): return jnp.sum(lax.all_gather(inp, lane_axis), axis=0)]
  transfers between devices with their start and end apart: 2 -> 1, of which waited for: 2 -> 1; matrix products, arithmetic and copies ran while one was open for 1% -> 1% of each run, Pallas kernels for 0% -> 0%
where the time goes in v1:
time: 686 us; the launch traced here: 683 us
  matrix products  356 us (52%)
  waiting for transfers between devices  181 us (26%)
  local copies, waits for them, and re-layouts  108 us (16%)
  blocking collectives  23 us (3%)
  between operations  13.5 us (2%)
    dot_general x16, matrix products, apply_group(): jnp.einsum('rgkt,rgkad->tad', onehot, product, precision=lax.Precision.HI...  233 us
    all_gather x1, waiting for transfers between devices, shards(): piece = lax.all_gather(mine, 'blk', axis=1, tiled=True)  181 us
    dot_general x16, matrix products, apply_group(): jnp.einsum('rgkab,rgkbd->rgkad', weights, picked, preferred_element_type=...  71.3 us
    dynamic_slice x16, local copies, waits for them, and re-layouts, fetch(): lax.dynamic_slice_in_dim(piece, offset * block_rows, group * block_rows, 1)  49.2 us
    reshape x16, local copies, waits for them, and re-layouts, apply_group(): hidden_group.reshape(rel_dev, group, tiles_block, tile_size * width)  42 us
    dot_general x16, matrix products, apply_group(): jnp.einsum('rgks,rgsx->rgkx', pick_cols, flat_hidden, preferred_element_t...  28.2 us
    dot_general x16, matrix products, apply_group(): jnp.einsum('rgkp,rpx->rgkx', pick_ids, pool_flat, preferred_element_type=...  20.7 us
  transfers between devices with their start and end apart: 1, of which 1 were waited for; matrix products, arithmetic and copies ran while one was open for 1% of the time, Pallas kernels for 0%

profile of v1, /device:TPU:1, one launch (start us, length us, event | category | flops | bytes accessed | tf_op | source)
XLA Modules:
  0.0 683.5 jit_solution(18112144711508040818)
XLA Ops:
  8.7 13.2 %all_to_all.18 = bf16[8,256,128]{1,2,0:T(8,128)(2,1)S(1)} all-to-all(bf16[8,256,128]{1,2,0:T(8,128)(2,1)S(1)} %fusion.31), channel_id=1, replica_groups=mesh['chan'=2,'blk'=64] {'chan'}, dimensions={0} | all-to-all | bytes 1048576 | tf_op jit(solution)/shard_map/all_to_all | solution.py:69
  23.0 7.3 %reshape_squeeze.3 = bf16[4,32,16384]{2,1,0:T(8,128)(2,1)} reshape(bf16[4,1,32,128,128]{4,3,2,1,0:T(8,128)(2,1)} %param.17) | data formatting | bytes 8388608 | tf_op jit(solution)/shard_map/reshape;squeeze | solution.py:34
  30.7 181.1 %all-gather.2.cloned.1.call-done = bf16[4,32768,128]{2,1,0:T(8,128)(2,1)} async-done(((bf16[4,512,128]{2,1,0:T(8,128)(2,1)}), bf16[4,32768,128]{2,1,0:T(8,128)(2,1)}) %all-gather.2.cloned.1.call-update) | async-done | bytes 33554448 | tf_op jit(solution)/shard_map/all_gather | solution.py:70
  211.9 454.1 %while.17 = (s32[]{:T(128)}, f32[4,128,128]{2,0,1:T(4,128)S(1)}, s32[4,64,8]{2,0,1:T(4,128)S(1)}, s32[4,64]{0,1:T(8,128)S(1)}, s32[4,64,8]{2,1,0:T(8,128)S(1)}, ...) while((s32[]{:T(128)}, f32[4,128,128]{2,0,1:T(4,128)S(1)}, ...), condition=%wide.region_1.0_spmd.clone.clone, body=%wide.region_0.0_spmd.clone.clone.sunk | while | flops 792860416 | bytes 65542100 | solution.py:83
  221.1 4.5 fusion.61
  225.6 14.6 %fusion.63 = f32[4,128,128]{2,0,1:T(4,128)S(1)} fusion(f32[4,4,8,128,128]{4,3,2,1,0:T(8,128)} %fusion.61, f32[4,128,128]{2,0,1:T(4,128)S(1)} %get-tuple-element.418, pred[]{:T(512)S(6)} %compare.3, f32[4,4,8]{2,0,1:T(4,128)S(1)} %fusion.62, s32[4,4,8]{2,0,1:T(4,128)S(1)} %get-tuple-element.402), kind=kOutput, calls=%fused_computation.14.clone.1 | convolution fusion | flops 100795392 | bytes 8913921 | tf_op jit(solution)/shard_map/while/body/eval_jaxpr/rgkt,rgkad->tad/dot_general | solution.py:61
  249.5 4.5 fusion.61
  254.0 14.6 %fusion.63 = f32[4,128,128]{2,0,1:T(4,128)S(1)} fusion(f32[4,4,8,128,128]{4,3,2,1,0:T(8,128)} %fusion.61, f32[4,128,128]{2,0,1:T(4,128)S(1)} %get-tuple-element.418, pred[]{:T(512)S(6)} %compare.3, f32[4,4,8]{2,0,1:T(4,128)S(1)} %fusion.62, s32[4,4,8]{2,0,1:T(4,128)S(1)} %get-tuple-element.402), kind=kOutput, calls=%fused_computation.14.clone.1 | convolution fusion | flops 100795392 | bytes 8913921 | tf_op jit(solution)/shard_map/while/body/eval_jaxpr/rgkt,rgkad->tad/dot_general | solution.py:61
  277.9 4.5 fusion.61
  282.4 14.6 %fusion.63 = f32[4,128,128]{2,0,1:T(4,128)S(1)} fusion(f32[4,4,8,128,128]{4,3,2,1,0:T(8,128)} %fusion.61, f32[4,128,128]{2,0,1:T(4,128)S(1)} %get-tuple-element.418, pred[]{:T(512)S(6)} %compare.3, f32[4,4,8]{2,0,1:T(4,128)S(1)} %fusion.62, s32[4,4,8]{2,0,1:T(4,128)S(1)} %get-tuple-element.402), kind=kOutput, calls=%fused_computation.14.clone.1 | convolution fusion | flops 100795392 | bytes 8913921 | tf_op jit(solution)/shard_map/while/body/eval_jaxpr/rgkt,rgkad->tad/dot_general | solution.py:61
  310.8 14.6 %fusion.63 = f32[4,128,128]{2,0,1:T(4,128)S(1)} fusion(f32[4,4,8,128,128]{4,3,2,1,0:T(8,128)} %fusion.61, f32[4,128,128]{2,0,1:T(4,128)S(1)} %get-tuple-element.418, pred[]{:T(512)S(6)} %compare.3, f32[4,4,8]{2,0,1:T(4,128)S(1)} %fusion.62, s32[4,4,8]{2,0,1:T(4,128)S(1)} %get-tuple-element.402), kind=kOutput, calls=%fused_computation.14.clone.1 | convolution fusion | flops 100795392 | bytes 8913921 | tf_op jit(solution)/shard_map/while/body/eval_jaxpr/rgkt,rgkad->tad/dot_general | solution.py:61
  334.6 4.5 fusion.61
  339.2 14.6 %fusion.63 = f32[4,128,128]{2,0,1:T(4,128)S(1)} fusion(f32[4,4,8,128,128]{4,3,2,1,0:T(8,128)} %fusion.61, f32[4,128,128]{2,0,1:T(4,128)S(1)} %get-tuple-element.418, pred[]{:T(512)S(6)} %compare.3, f32[4,4,8]{2,0,1:T(4,128)S(1)} %fusion.62, s32[4,4,8]{2,0,1:T(4,128)S(1)} %get-tuple-element.402), kind=kOutput, calls=%fused_computation.14.clone.1 | convolution fusion | flops 100795392 | bytes 8913921 | tf_op jit(solution)/shard_map/while/body/eval_jaxpr/rgkt,rgkad->tad/dot_general | solution.py:61
  363.0 4.5 fusion.61
  367.5 14.6 %fusion.63 = f32[4,128,128]{2,0,1:T(4,128)S(1)} fusion(f32[4,4,8,128,128]{4,3,2,1,0:T(8,128)} %fusion.61, f32[4,128,128]{2,0,1:T(4,128)S(1)} %get-tuple-element.418, pred[]{:T(512)S(6)} %compare.3, f32[4,4,8]{2,0,1:T(4,128)S(1)} %fusion.62, s32[4,4,8]{2,0,1:T(4,128)S(1)} %get-tuple-element.402), kind=kOutput, calls=%fused_computation.14.clone.1 | convolution fusion | flops 100795392 | bytes 8913921 | tf_op jit(solution)/shard_map/while/body/eval_jaxpr/rgkt,rgkad->tad/dot_general | solution.py:61
  391.4 4.5 fusion.61
  395.9 14.6 %fusion.63 = f32[4,128,128]{2,0,1:T(4,128)S(1)} fusion(f32[4,4,8,128,128]{4,3,2,1,0:T(8,128)} %fusion.61, f32[4,128,128]{2,0,1:T(4,128)S(1)} %get-tuple-element.418, pred[]{:T(512)S(6)} %compare.3, f32[4,4,8]{2,0,1:T(4,128)S(1)} %fusion.62, s32[4,4,8]{2,0,1:T(4,128)S(1)} %get-tuple-element.402), kind=kOutput, calls=%fused_computation.14.clone.1 | convolution fusion | flops 100795392 | bytes 8913921 | tf_op jit(solution)/shard_map/while/body/eval_jaxpr/rgkt,rgkad->tad/dot_general | solution.py:61
  424.3 14.6 %fusion.63 = f32[4,128,128]{2,0,1:T(4,128)S(1)} fusion(f32[4,4,8,128,128]{4,3,2,1,0:T(8,128)} %fusion.61, f32[4,128,128]{2,0,1:T(4,128)S(1)} %get-tuple-element.418, pred[]{:T(512)S(6)} %compare.3, f32[4,4,8]{2,0,1:T(4,128)S(1)} %fusion.62, s32[4,4,8]{2,0,1:T(4,128)S(1)} %get-tuple-element.402), kind=kOutput, calls=%fused_computation.14.clone.1 | convolution fusion | flops 100795392 | bytes 8913921 | tf_op jit(solution)/shard_map/while/body/eval_jaxpr/rgkt,rgkad->tad/dot_general | solution.py:61
  448.1 4.5 fusion.61
  452.7 14.6 %fusion.63 = f32[4,128,128]{2,0,1:T(4,128)S(1)} fusion(f32[4,4,8,128,128]{4,3,2,1,0:T(8,128)} %fusion.61, f32[4,128,128]{2,0,1:T(4,128)S(1)} %get-tuple-element.418, pred[]{:T(512)S(6)} %compare.3, f32[4,4,8]{2,0,1:T(4,128)S(1)} %fusion.62, s32[4,4,8]{2,0,1:T(4,128)S(1)} %get-tuple-element.402), kind=kOutput, calls=%fused_computation.14.clone.1 | convolution fusion | flops 100795392 | bytes 8913921 | tf_op jit(solution)/shard_map/while/body/eval_jaxpr/rgkt,rgkad->tad/dot_general | solution.py:61
  481.1 14.6 %fusion.63 = f32[4,128,128]{2,0,1:T(4,128)S(1)} fusion(f32[4,4,8,128,128]{4,3,2,1,0:T(8,128)} %fusion.61, f32[4,128,128]{2,0,1:T(4,128)S(1)} %get-tuple-element.418, pred[]{:T(512)S(6)} %compare.3, f32[4,4,8]{2,0,1:T(4,128)S(1)} %fusion.62, s32[4,4,8]{2,0,1:T(4,128)S(1)} %get-tuple-element.402), kind=kOutput, calls=%fused_computation.14.clone.1 | convolution fusion | flops 100795392 | bytes 8913921 | tf_op jit(solution)/shard_map/while/body/eval_jaxpr/rgkt,rgkad->tad/dot_general | solution.py:61
  504.9 4.5 fusion.61
  509.4 14.6 %fusion.63 = f32[4,128,128]{2,0,1:T(4,128)S(1)} fusion(f32[4,4,8,128,128]{4,3,2,1,0:T(8,128)} %fusion.61, f32[4,128,128]{2,0,1:T(4,128)S(1)} %get-tuple-element.418, pred[]{:T(512)S(6)} %compare.3, f32[4,4,8]{2,0,1:T(4,128)S(1)} %fusion.62, s32[4,4,8]{2,0,1:T(4,128)S(1)} %get-tuple-element.402), kind=kOutput, calls=%fused_computation.14.clone.1 | convolution fusion | flops 100795392 | bytes 8913921 | tf_op jit(solution)/shard_map/while/body/eval_jaxpr/rgkt,rgkad->tad/dot_general | solution.py:61
  533.3 4.5 fusion.61
  537.8 14.6 %fusion.63 = f32[4,128,128]{2,0,1:T(4,128)S(1)} fusion(f32[4,4,8,128,128]{4,3,2,1,0:T(8,128)} %fusion.61, f32[4,128,128]{2,0,1:T(4,128)S(1)} %get-tuple-element.418, pred[]{:T(512)S(6)} %compare.3, f32[4,4,8]{2,0,1:T(4,128)S(1)} %fusion.62, s32[4,4,8]{2,0,1:T(4,128)S(1)} %get-tuple-element.402), kind=kOutput, calls=%fused_computation.14.clone.1 | convolution fusion | flops 100795392 | bytes 8913921 | tf_op jit(solution)/shard_map/while/body/eval_jaxpr/rgkt,rgkad->tad/dot_general | solution.py:61
  561.7 4.5 fusion.61
  566.2 14.6 %fusion.63 = f32[4,128,128]{2,0,1:T(4,128)S(1)} fusion(f32[4,4,8,128,128]{4,3,2,1,0:T(8,128)} %fusion.61, f32[4,128,128]{2,0,1:T(4,128)S(1)} %get-tuple-element.418, pred[]{:T(512)S(6)} %compare.3, f32[4,4,8]{2,0,1:T(4,128)S(1)} %fusion.62, s32[4,4,8]{2,0,1:T(4,128)S(1)} %get-tuple-element.402), kind=kOutput, calls=%fused_computation.14.clone.1 | convolution fusion | flops 100795392 | bytes 8913921 | tf_op jit(solution)/shard_map/while/body/eval_jaxpr/rgkt,rgkad->tad/dot_general | solution.py:61
  594.6 14.6 %fusion.63 = f32[4,128,128]{2,0,1:T(4,128)S(1)} fusion(f32[4,4,8,128,128]{4,3,2,1,0:T(8,128)} %fusion.61, f32[4,128,128]{2,0,1:T(4,128)S(1)} %get-tuple-element.418, pred[]{:T(512)S(6)} %compare.3, f32[4,4,8]{2,0,1:T(4,128)S(1)} %fusion.62, s32[4,4,8]{2,0,1:T(4,128)S(1)} %get-tuple-element.402), kind=kOutput, calls=%fused_computation.14.clone.1 | convolution fusion | flops 100795392 | bytes 8913921 | tf_op jit(solution)/shard_map/while/body/eval_jaxpr/rgkt,rgkad->tad/dot_general | solution.py:61
  618.4 4.5 fusion.61
  623.0 14.6 %fusion.63 = f32[4,128,128]{2,0,1:T(4,128)S(1)} fusion(f32[4,4,8,128,128]{4,3,2,1,0:T(8,128)} %fusion.61, f32[4,128,128]{2,0,1:T(4,128)S(1)} %get-tuple-element.418, pred[]{:T(512)S(6)} %compare.3, f32[4,4,8]{2,0,1:T(4,128)S(1)} %fusion.62, s32[4,4,8]{2,0,1:T(4,128)S(1)} %get-tuple-element.402), kind=kOutput, calls=%fused_computation.14.clone.1 | convolution fusion | flops 100795392 | bytes 8913921 | tf_op jit(solution)/shard_map/while/body/eval_jaxpr/rgkt,rgkad->tad/dot_general | solution.py:61
  651.3 14.6 %fusion.63 = f32[4,128,128]{2,0,1:T(4,128)S(1)} fusion(f32[4,4,8,128,128]{4,3,2,1,0:T(8,128)} %fusion.61, f32[4,128,128]{2,0,1:T(4,128)S(1)} %get-tuple-element.418, pred[]{:T(512)S(6)} %compare.3, f32[4,4,8]{2,0,1:T(4,128)S(1)} %fusion.62, s32[4,4,8]{2,0,1:T(4,128)S(1)} %get-tuple-element.402), kind=kOutput, calls=%fused_computation.14.clone.1 | convolution fusion | flops 100795392 | bytes 8913921 | tf_op jit(solution)/shard_map/while/body/eval_jaxpr/rgkt,rgkad->tad/dot_general | solution.py:61
  666.0 9.8 %all_gather.7 = f32[2,512,128]{2,1,0:T(8,128)S(1)} all-gather(f32[1,512,128]{2,1,0:T(8,128)S(1)} %bitcast.61), channel_id=1, replica_groups=mesh['chan'=2,'blk'=64] {'chan'}, dimensions={0}, use_global_device_ids=true | all-gather | bytes 786432 | tf_op jit(solution)/shard_map/all_gather | solution.py:10
  (191 shorter events, 174.7 us)
Async XLA Ops:
  6.5 1.0 copy-start
  6.5 205.3 %all-gather.2.cloned.1.call-start = ((), (), s32[]{:S(2)}) async-start(), calls=%async_computation.1 | async-start | bytes 34078720 | tf_op jit(solution)/shard_map/all_gather | solution.py:70
  22.9 7.3 %copy-start.4 = (s32[4,1,64,8]{2,3,1,0:T(8,128)S(1)}, s32[4,1,64,8]{2,3,1,0:T(8,128)}, u32[]{:S(2)}) copy-start(s32[4,1,64,8]{2,3,1,0:T(8,128)} %param.13) | copy-start | bytes 24580
  22.9 7.4 %copy-start.5 = (s32[4,1,64,8]{2,3,1,0:T(8,128)S(1)}, s32[4,1,64,8]{2,3,1,0:T(8,128)}, u32[]{:S(2)}) copy-start(s32[4,1,64,8]{2,3,1,0:T(8,128)} %param.15) | copy-start | bytes 24580
  22.9 7.5 %copy-start.6 = (s32[4,1,64,8]{2,3,1,0:T(8,128)S(1)}, s32[4,1,64,8]{2,3,1,0:T(8,128)}, u32[]{:S(2)}) copy-start(s32[4,1,64,8]{2,3,1,0:T(8,128)} %param.14) | copy-start | bytes 24580
  23.0 7.7 %copy-start.7 = (s32[4,1,64]{2,1,0:T(1,128)S(1)}, s32[4,1,64]{2,1,0:T(1,128)}, u32[]{:S(2)}) copy-start(s32[4,1,64]{2,1,0:T(1,128)} %param.16) | copy-start | bytes 3076
  211.9 464.0 %copy-start.2 = (bf16[1,1,256,128]{3,2,1,0:T(8,128)(2,1)S(1)}, bf16[1,1,256,128]{3,2,1,0:T(8,128)(2,1)}, u32[]{:S(2)}) copy-start(bf16[1,1,256,128]{3,2,1,0:T(8,128)(2,1)} %param.10) | copy-start | bytes 196612
  211.9 464.0 %copy-start.3 = (bf16[128,128]{1,0:T(8,128)(2,1)S(1)}, bf16[128,128]{1,0:T(8,128)(2,1)}, u32[]{:S(2)}) copy-start(bf16[128,128]{1,0:T(8,128)(2,1)} %param.12) | copy-start | bytes 98308
  217.6 2.2 copy-start.1
  246.0 2.2 copy-start.1
  274.4 2.2 copy-start.1
  302.8 2.2 copy-start.1
  331.1 2.2 copy-start.1
  359.5 2.2 copy-start.1
  387.9 2.2 copy-start.1
  416.3 2.2 copy-start.1
  444.6 2.2 copy-start.1
  473.0 2.2 copy-start.1
  501.4 2.2 copy-start.1
  529.8 2.2 copy-start.1
  558.2 2.2 copy-start.1
  586.6 2.2 copy-start.1
  614.9 2.2 copy-start.1
  643.3 2.2 copy-start.1
Sparse Core Ops, SparseCore 0:
  23.0 188.7 all-gather.1
